TPU v7x, 32 devices: a whole 2x2x4 slice. The times are simulated.
32 devices in a mesh: patch: 2 (over x), epoch: 16 (over z, y, core).
Axes of the slice: x: 2, y: 2, z: 4, core: 2. Of those that a mesh axis runs over, the one named last changes fastest.
Arguments:
- images: float32 [32, 128, 1024], P(('patch', 'epoch')), parts along dimension 0, may hold values from -20 to 20, as said below
- variance: float32 [32], P(('patch', 'epoch')), parts along dimension 0, may hold values from 0.25 to 4
- zero_point: float32 [32], P(('patch', 'epoch')), parts along dimension 0, may hold values from 0.5 to 2
- block_mask: int32 [32, 1], P(('patch', 'epoch')), parts along dimension 0, may hold values 0 or 1
- stamps: int32 [32, 512], P(('patch', 'epoch')), parts along dimension 0, may hold values from 0 to 131071
- owners: int32 [8], P('patch'), parts along dimension 0, may hold values from 0 to 15
Outputs:
- significance: float32 [32, 128, 1024], P(('patch', 'epoch')), parts along dimension 0
- coefficients: float32 [32, 15], P(('patch', 'epoch')), parts along dimension 0
There are 2 independent parts, one for each index of `patch`. A program takes and returns all parts, laid end to end along the dimension named above; each array names one. Nothing has to cross between parts.
Inputs may be any that keep to these rules, and one draw needn't show every extreme that they name: `images`: each epoch is a common sky times an epoch scale plus noise.
All inputs are finite; a program needn't handle non-finite values. No bound on the sum of `block_mask` on one device may be relied on, other than what follows from the above.
Results may differ from a plain program's by a relative error of at most 0.00075.
The roundings to bfloat16 on the way count: a program that leaves them out, or rounds other values in their place, can miss the bound.
Values sent between devices are 32-bit elements; how exact they have to be, the bound alone decides.
A program may use at most 64 MiB of HBM per device.

v0:
```python
import math

import jax
import jax.numpy as jnp
from jax import lax
from jax.sharding import PartitionSpec as P

TILES = 4
KHALF = 7
NBASIS = 12


sigma_list = (0.75, 1.5, 3.0)
basis_pairs = ((0, 0), (2, 0), (0, 2), (1, 1))


def raise_power(scaled, degree):
    result = jnp.ones_like(scaled)
    for step in range(degree):
        result = result * scaled
    return result


def tap_values(offset, sigma, degree):
    scaled = offset / sigma
    value = (
        jnp.exp(-0.5 * scaled * scaled)
        * raise_power(scaled, degree)
        / (math.sqrt(2.0 * math.pi) * sigma)
    )
    value = jnp.where(jnp.abs(offset) <= KHALF, value, 0.0)
    return value.astype(jnp.bfloat16)


def band_matrix(count, sigma, degree, along_cols):
    index = jnp.arange(count, dtype=jnp.int32)
    if along_cols:
        offset = index[:, None] - index[None, :]
    else:
        offset = index[None, :] - index[:, None]
    return tap_values(offset.astype(jnp.float32), sigma, degree)


def shards(images, variance, zero_point, block_mask, stamps, owners):
    image = images[0]
    rows_all, cols_all = image.shape
    count = lax.axis_size("epoch")
    weight = 1.0 / variance[0]
    mask_f = block_mask[0].astype(jnp.float32)
    block_term = weight * mask_f
    numer = jnp.repeat(block_term, 128)[:, None] * image
    scales_all = lax.all_gather(zero_point, "epoch", axis=0, tiled=True)
    owner_scale = jnp.sum(
        (owners[:, None] == jnp.arange(count)[None, :]).astype(jnp.float32) * scales_all[None, :],
        axis=1,
    )
    col_scale = jnp.repeat(owner_scale, cols_all // TILES)
    stamp_row = stamps[0]
    numer_sum, block_sum = lax.psum((numer, block_term), "epoch")
    den_rows = jnp.repeat(1.0 + block_sum, 128)
    reference_img = numer_sum / den_rows[:, None] * col_scale[None, :]
    stamp_ref = jnp.take(reference_img.reshape(-1), stamp_row)
    sharp = image.astype(jnp.bfloat16)
    bases = []
    for sigma in sigma_list:
        across = {}
        for degree in (0, 1, 2):
            across[degree] = jnp.dot(
                sharp,
                band_matrix(cols_all, sigma, degree, True),
                preferred_element_type=jnp.float32,
            ).astype(jnp.bfloat16)
        for pair in basis_pairs:
            vertical = band_matrix(rows_all, sigma, pair[1], False)
            bases.append(
                jnp.dot(vertical, across[pair[0]], preferred_element_type=jnp.float32).astype(
                    jnp.bfloat16
                )
            )
    xn = 2.0 * (jnp.arange(cols_all).astype(jnp.float32) + 0.5) / cols_all - 1.0
    yn = 2.0 * (jnp.arange(rows_all).astype(jnp.float32) + 0.5) / rows_all - 1.0
    picks = [jnp.take(b.reshape(-1), stamp_row).astype(jnp.float32) for b in bases]
    picks = picks + [
        jnp.ones(stamp_row.shape, jnp.float32),
        xn[stamp_row % cols_all],
        yn[stamp_row // cols_all],
    ]
    design = jnp.stack(picks, axis=0)
    normal = jnp.dot(design, design.T, precision=lax.Precision.HIGHEST)
    normal = normal + 0.05 * jnp.diag(jnp.diag(normal))
    rhs = jnp.dot(design, stamp_ref, precision=lax.Precision.HIGHEST)
    factor = jnp.linalg.cholesky(normal)
    coef = jax.scipy.linalg.cho_solve((factor, True), rhs)
    model = jnp.zeros((rows_all, cols_all), jnp.float32)
    for index in range(NBASIS):
        model = model + coef[index] * bases[index].astype(jnp.float32)
    model = model + coef[NBASIS] + coef[NBASIS + 1] * xn[None, :] + coef[NBASIS + 2] * yn[:, None]
    diff = jnp.repeat(mask_f, 128)[:, None] * (model - reference_img)
    pooled = lax.psum(diff * diff, "epoch")
    scatter = jnp.sqrt(0.05 + pooled / count)
    result = diff / scatter
    return (result[None], coef[None])


def solution(mesh):
    in_specs = (
        P(("patch", "epoch"), None, None),
        P(("patch", "epoch")),
        P(("patch", "epoch")),
        P(("patch", "epoch"), None),
        P(("patch", "epoch"), None),
        P("patch"),
    )
    out_specs = (P(("patch", "epoch"), None, None), P(("patch", "epoch"), None))
    return jax.shard_map(shards, mesh=mesh, in_specs=in_specs, out_specs=out_specs, check_vma=False)
```

profile of v0, /device:TPU:0, one launch (start us, length us, event | category | flops | bytes accessed | tf_op | source)
XLA Modules:
  0.0 242.0 jit_solution(10815017619409974044)
XLA Ops:
  8.5 2.2 fusion.182
  10.8 2.3 fusion.11
  13.1 2.2 fusion.15
  15.3 2.4 fusion.14
  18.2 2.3 fusion.18
  20.5 2.2 fusion.22
  22.6 2.6 %fusion.21 = bf16[128,1024]{1,0:T(8,128)(2,1)S(1)} fusion(bf16[1,128,1024]{2,1,0:T(8,128)(2,1)S(1)} %get-tuple-element.11), kind=kOutput, calls=%fused_computation.54 | convolution fusion | flops 314998784 | bytes 524288 | tf_op jit(solution)/shard_map/dot_general | solution.py:76
  25.7 3.0 %fusion.25 = bf16[128,1024]{1,0:T(8,128)(2,1)} fusion(bf16[1,128,1024]{2,1,0:T(8,128)(2,1)S(1)} %get-tuple-element.11), kind=kOutput, calls=%fused_computation.58 | convolution fusion | flops 313966592 | bytes 524288 | tf_op jit(solution)/shard_map/dot_general | solution.py:76
  28.7 2.2 fusion.29
  30.9 3.1 %fusion.28 = bf16[128,1024]{1,0:T(8,128)(2,1)} fusion(bf16[1,128,1024]{2,1,0:T(8,128)(2,1)S(1)} %get-tuple-element.11), kind=kOutput, calls=%fused_computation.61 | convolution fusion | flops 314998784 | bytes 524288 | tf_op jit(solution)/shard_map/dot_general | solution.py:76
  36.5 36.3 %all-reduce.1 = (f32[16]{0:T(128)S(1)}, f32[1]{0:T(128)}) all-reduce(f32[16]{0:T(128)S(1)} %dynamic-update-slice.3, f32[1]{0:T(128)} %mul.385), channel_id=1, replica_groups=mesh['patch'=2,'epoch'=16] {'epoch'}, use_global_device_ids=true, to_apply=%add | all-reduce | flops 17 | bytes 136
  73.9 3.5 %gather_fusion.15 = bf16[512]{0:T(512)(128)(2,1)S(1)} fusion(bf16[131072]{0:T(1024)(128)(2,1)S(1)} %bitcast.149, s32[1024]{0:T(1024)S(1)} %pad_clamp_fusion.3), kind=kCustom, calls=%fused_computation.11.clone | custom fusion | bytes 4096 | tf_op jit(solution)/shard_map/jit(_take)/gather | solution.py:82
  77.4 3.5 %gather_fusion.14 = bf16[512]{0:T(512)(128)(2,1)S(1)} fusion(bf16[131072]{0:T(1024)(128)(2,1)S(1)} %bitcast.148, s32[1024]{0:T(1024)S(1)} %pad_clamp_fusion.3), kind=kCustom, calls=%fused_computation.10.clone | custom fusion | bytes 4096 | tf_op jit(solution)/shard_map/jit(_take)/gather | solution.py:82
  81.0 3.5 %gather_fusion.13 = bf16[512]{0:T(512)(128)(2,1)S(1)} fusion(bf16[131072]{0:T(1024)(128)(2,1)S(1)} %bitcast.151, s32[1024]{0:T(1024)S(1)} %pad_clamp_fusion.3), kind=kCustom, calls=%fused_computation.9.clone | custom fusion | bytes 4096 | tf_op jit(solution)/shard_map/jit(_take)/gather | solution.py:82
  84.6 3.5 %gather_fusion.12 = bf16[512]{0:T(512)(128)(2,1)S(1)} fusion(bf16[131072]{0:T(1024)(128)(2,1)S(1)} %bitcast.152, s32[1024]{0:T(1024)S(1)} %pad_clamp_fusion.3), kind=kCustom, calls=%fused_computation.8.clone | custom fusion | bytes 4096 | tf_op jit(solution)/shard_map/jit(_take)/gather | solution.py:82
  88.1 3.5 %gather_fusion.11 = bf16[512]{0:T(512)(128)(2,1)S(1)} fusion(bf16[131072]{0:T(1024)(128)(2,1)S(1)} %bitcast.153, s32[1024]{0:T(1024)S(1)} %pad_clamp_fusion.3), kind=kCustom, calls=%fused_computation.7.clone | custom fusion | bytes 4096 | tf_op jit(solution)/shard_map/jit(_take)/gather | solution.py:82
  91.7 3.5 %gather_fusion.10 = bf16[512]{0:T(512)(128)(2,1)S(1)} fusion(bf16[131072]{0:T(1024)(128)(2,1)S(1)} %bitcast.154, s32[1024]{0:T(1024)S(1)} %pad_clamp_fusion.3), kind=kCustom, calls=%fused_computation.6.clone | custom fusion | bytes 4096 | tf_op jit(solution)/shard_map/jit(_take)/gather | solution.py:82
  95.3 3.5 %gather_fusion.9 = bf16[512]{0:T(512)(128)(2,1)S(1)} fusion(bf16[131072]{0:T(1024)(128)(2,1)S(1)} %bitcast.155, s32[1024]{0:T(1024)S(1)} %pad_clamp_fusion.3), kind=kCustom, calls=%fused_computation.5.clone | custom fusion | bytes 4096 | tf_op jit(solution)/shard_map/jit(_take)/gather | solution.py:82
  98.9 3.5 %gather_fusion.8 = bf16[512]{0:T(512)(128)(2,1)S(1)} fusion(bf16[131072]{0:T(1024)(128)(2,1)S(1)} %bitcast.156, s32[1024]{0:T(1024)S(1)} %pad_clamp_fusion.3), kind=kCustom, calls=%fused_computation.4.clone | custom fusion | bytes 4096 | tf_op jit(solution)/shard_map/jit(_take)/gather | solution.py:82
  102.5 3.5 %gather_fusion.7 = bf16[512]{0:T(512)(128)(2,1)S(1)} fusion(bf16[131072]{0:T(1024)(128)(2,1)S(1)} %bitcast.157, s32[1024]{0:T(1024)S(1)} %pad_clamp_fusion.3), kind=kCustom, calls=%fused_computation.3.clone | custom fusion | bytes 4096 | tf_op jit(solution)/shard_map/jit(_take)/gather | solution.py:82
  106.0 3.5 %gather_fusion.6 = bf16[512]{0:T(512)(128)(2,1)S(1)} fusion(bf16[131072]{0:T(1024)(128)(2,1)S(1)} %bitcast.158, s32[1024]{0:T(1024)S(1)} %pad_clamp_fusion.3), kind=kCustom, calls=%fused_computation.2.clone | custom fusion | bytes 4096 | tf_op jit(solution)/shard_map/jit(_take)/gather | solution.py:82
  109.6 3.5 %gather_fusion.5 = bf16[512]{0:T(512)(128)(2,1)S(1)} fusion(bf16[131072]{0:T(1024)(128)(2,1)S(1)} %bitcast.159, s32[1024]{0:T(1024)S(1)} %pad_clamp_fusion.3), kind=kCustom, calls=%fused_computation.1.clone | custom fusion | bytes 4096 | tf_op jit(solution)/shard_map/jit(_take)/gather | solution.py:82
  113.2 3.5 %gather_fusion.4 = bf16[512]{0:T(512)(128)(2,1)S(1)} fusion(bf16[131072]{0:T(1024)(128)(2,1)S(1)} %bitcast.150, s32[1024]{0:T(1024)S(1)} %pad_clamp_fusion.3), kind=kCustom, calls=%fused_computation.clone | custom fusion | bytes 4096 | tf_op jit(solution)/shard_map/jit(_take)/gather | solution.py:82
  116.7 2.3 gather_fusion
  119.0 3.3 %gather_fusion.1 = f32[512]{0:T(512)S(1)} fusion(f32[128]{0:T(128)S(1)} %multiply_add_fusion.1, s32[1024]{0:T(1024)S(1)} %pad_clamp_fusion.1), kind=kCustom, calls=%fused_computation.13 | custom fusion | bytes 6144 | tf_op jit(solution)/shard_map/gather | solution.py:86
  122.4 1.1 fusion.45
  123.6 3.1 %gather_fusion.3 = f32[512]{0:T(512)S(1)} fusion(f32[131072]{0:T(1024)S(1)} %bitcast.147, s32[1024]{0:T(1024)S(1)} %pad_clamp_fusion), kind=kCustom, calls=%fused_computation.15 | custom fusion | bytes 6144 | tf_op jit(solution)/shard_map/jit(_take)/gather | solution.py:62
  128.1 1.4 cholesky.16
  130.8 1.2 custom-call.10
  134.3 10.7 %fusion.181 = (f32[128,1024]{1,0:T(8,128)}, f32[128,1024]{1,0:T(8,128)S(1)}) fusion(f32[1024]{0:T(1024)S(1)} %bitcast.174, f32[128,1024]{1,0:T(8,128)S(1)} %copy-done, f32[]{:T(128)} %bitcast.27, f32[128]{0:T(128)S(1)} %broadcast_multiply_fusion.1, f32[1024]{0:T(1024)S(1)} %broadcast_multiply_fusion, f32[]{:T(128)} %bitcast.48, ...), kind=kLoop, calls=%fused_computation.250 | loop fusion | flops 5636096 | bytes 4727356 | tf_op jit(solution)/shard_map/mul | solution.py:99
  145.0 88.2 %all-reduce.7.cloned.1.call-done = f32[128,1024]{1,0:T(8,128)} async-done(((f32[128,1024]{1,0:T(8,128)}), f32[128,1024]{1,0:T(8,128)}) %all-reduce.7.cloned.1.call-update) | async-done | bytes 524304 | tf_op jit(solution)/shard_map/psum | solution.py:99
  233.2 1.9 multiply_bitcast_fusion
  (73 shorter events, 8.8 us)
Async XLA Ops:
  7.2 115.3 %all-reduce.5.cloned.1.call-start = ((), (), s32[]{:S(2)}) async-start(), calls=%async_computation | async-start | bytes 1048576 | tf_op jit(solution)/shard_map/psum | solution.py:59
  10.8 222.4 %all-reduce.7.cloned.1.call-start = ((), (), s32[]{:S(2)}) async-start(), calls=%async_computation.1 | async-start | bytes 1048576 | tf_op jit(solution)/shard_map/psum | solution.py:99
  25.2 70.0 %copy-start.1 = (bf16[128,1024]{1,0:T(8,128)(2,1)}, bf16[128,1024]{1,0:T(8,128)(2,1)S(1)}, u32[]{:S(2)}) copy-start(bf16[128,1024]{1,0:T(8,128)(2,1)S(1)} %fusion.21) | copy-start | bytes 786436
  34.0 1.1 copy-start.7
  34.0 38.8 %copy-start.6 = (s32[4]{0:T(128)S(1)}, s32[4]{0:T(128)}, u32[]{:S(2)}) copy-start(s32[4]{0:T(128)} %param.13) | copy-start | bytes 52
  34.0 39.0 %copy-start.5 = (s32[1,512]{1,0:T(1,128)S(1)}, s32[1,512]{1,0:T(1,128)}, u32[]{:S(2)}) copy-start(s32[1,512]{1,0:T(1,128)} %param.12) | copy-start | bytes 6148
  98.9 3.5 %copy-start.2 = (bf16[128,1024]{1,0:T(8,128)(2,1)S(1)}, bf16[128,1024]{1,0:T(8,128)(2,1)}, u32[]{:S(2)}) copy-start(bf16[128,1024]{1,0:T(8,128)(2,1)} %fusion.25) | copy-start | bytes 786436
  106.0 3.5 %copy-start.3 = (bf16[128,1024]{1,0:T(8,128)(2,1)S(1)}, bf16[128,1024]{1,0:T(8,128)(2,1)}, u32[]{:S(2)}) copy-start(bf16[128,1024]{1,0:T(8,128)(2,1)} %fusion.28) | copy-start | bytes 786436
  126.8 7.5 %copy-start = (f32[128,1024]{1,0:T(8,128)S(1)}, f32[128,1024]{1,0:T(8,128)}, u32[]{:S(2)}) copy-start(f32[128,1024]{1,0:T(8,128)} %all-reduce.5.cloned.1.call-done) | copy-start | bytes 1572868
  132.3 12.7 %copy-start.4 = (f32[1,15]{1,0:T(1,128)}, f32[1,15]{1,0:T(1,128)S(1)}, u32[]{:S(2)}) copy-start(f32[1,15]{1,0:T(1,128)S(1)} %fusion.71) | copy-start | bytes 184
Sparse Core Ops, SparseCore 0:
  11.9 93.5 all-reduce.4
  145.1 88.0 all-reduce.6
where the time goes:
time: 242 us
  waiting for transfers between devices  88.2 us (36%)
  local copies, waits for them, and re-layouts  54.6 us (23%)
  blocking collectives  36.3 us (15%)
  matrix products  24.1 us (10%)
  other arithmetic  21.4 us (9%)
  between operations  17.2 us (7%)
    psum x1, waiting for transfers between devices, shards(): pooled = lax.psum(diff * diff, 'epoch')  88.2 us
    gather x12, local copies, waits for them, and re-layouts, shards(): jnp.take(b.reshape(-1), stamp_row).astype(jnp.float32)  42.2 us
    unnamed x1, blocking collectives  36.3 us
    dot_general x12, matrix products, shards(): jnp.dot(vertical, across[pair[0]], preferred_element_type=jnp.float32)  17 us
    mul x1, other arithmetic, shards(): pooled = lax.psum(diff * diff, 'epoch')  10.7 us
    dot_general x3, matrix products, shards(): jnp.dot(sharp, band_matrix(cols_all, sigma, degree, True), preferred_elem...  6.5 us
  transfers between devices with their start and end apart: 2, of which 1 were waited for; matrix products, arithmetic and copies ran while one was open for 30% of the time, Pallas kernels for 0%

commit v1 on v0

v1 whole, which is shorter than its diff:
```python
import functools
import math

import jax
import jax.numpy as jnp
from jax import lax
from jax.experimental import pallas as pl
from jax.experimental.pallas import tpu as pltpu
from jax.sharding import PartitionSpec as P

TILES = 4
KHALF = 7
NBASIS = 12
CHUNKS = 2
LANES = 128

sigma_list = (0.75, 1.5, 3.0)
basis_pairs = ((0, 0), (2, 0), (0, 2), (1, 1))
MESH = pl.DeviceIdType.MESH


def tap_values(offset, sigma, degree):
    scaled = offset / sigma
    power = jnp.ones_like(scaled)
    for _ in range(degree):
        power = power * scaled
    value = jnp.exp(-0.5 * scaled * scaled) * power / (math.sqrt(2.0 * math.pi) * sigma)
    return jnp.where(jnp.abs(offset) <= KHALF, value, 0.0).astype(jnp.bfloat16)


def grid_of(count):
    chips = count // 2
    middle = 1
    while middle * 2 * middle * 2 <= chips:
        middle *= 2
    if chips % middle:
        middle = 1
    return chips // middle, middle


def kernel(
    count, height, width,
    image_ref, var_ref, zp_ref, mask_ref, owner_ref, stamp_ref,
    out_ref, coef_ref,
    x1, x2, g1, g2, ra1, ra2, rb1, rb2, rc1, rc2,
    s_own, s_mid, s_sum, sa, sb, sc,
    lhs, across, bases, onehot, design, diff_s,
    send1, recv1, send2, recv2, send3, recv3,
):
    zn, yn_count = grid_of(count)
    half = zn * yn_count
    chunks, _, pr, pcc = x1.shape
    subs = width // chunks // pcc
    groups = height // pr
    cw = width // chunks
    npix = stamp_ref.shape[1]

    me = lax.axis_index("epoch")
    core = lax.rem(me, 2)
    chip = me // 2
    y = lax.rem(chip, yn_count)
    z = chip // yn_count

    def device(zz, yy, cc):
        return {"epoch": (zz * yn_count + yy) * 2 + cc}

    mate = device(z, y, 1 - core)
    ys = [lax.rem(y + d, yn_count) for d in range(1, yn_count)]
    zs = [lax.rem(z + d, zn) for d in range(1, zn)]
    peers = [mate] + [device(z, yy, core) for yy in ys] + [device(zz, y, core) for zz in zs]
    mine = (core * yn_count + y) * zn + z

    barrier = pltpu.get_barrier_semaphore()
    for peer in peers:
        pl.semaphore_signal(barrier, inc=1, device_id=peer, device_id_type=MESH)

    pending = []

    class Lane:
        def __init__(self, send, recv):
            self.send, self.recv, self.next = send, recv, 0

        def start(self, src, dst, device_id):
            copy = pltpu.make_async_remote_copy(
                src_ref=src, dst_ref=dst, send_sem=self.send.at[self.next], recv_sem=self.recv.at[self.next],
                device_id=device_id, device_id_type=MESH,
            )
            self.next += 1
            copy.start()
            pending.append(copy)
            return copy

    class Reduce:
        def __init__(self, x, g, ra, rb, rc, lane):
            self.x, self.g, self.ra, self.rb, self.rc, self.lane = x, g, ra, rb, rc, lane
            self.at = {}

        def a(self, ch):
            self.at["a", ch] = [
                self.lane.start(self.x.at[ch, pl.ds((1 - core) * half, half)], self.ra.at[ch], mate)
            ]

        def wait(self, stage, ch):
            for copy in self.at[stage, ch]:
                copy.wait_recv()

        def b(self, ch):
            self.wait("a", ch)
            for i in range(half):
                self.x[ch, core * half + i] = self.x[ch, core * half + i] + self.ra[ch, i]
            self.at["b", ch] = [
                self.lane.start(
                    self.x.at[ch, pl.ds(core * half + yy * zn, zn)], self.rb.at[ch, d], device(z, yy, core)
                )
                for d, yy in enumerate(ys)
            ]

        def c(self, ch):
            self.wait("b", ch)
            base = core * half + y * zn
            for i in range(zn):
                total = self.x[ch, base + i]
                for d in range(yn_count - 1):
                    total = total + self.rb[ch, d, i]
                self.x[ch, base + i] = total
            self.at["c", ch] = [
                self.lane.start(self.x.at[ch, base + zz], self.rc.at[ch, d], device(zz, y, core))
                for d, zz in enumerate(zs)
            ]

        def d(self, ch, final):
            self.wait("c", ch)
            total = self.x[ch, mine]
            for d in range(zn - 1):
                total = total + self.rc[ch, d]
            self.g[ch, mine] = final(ch, total)
            self.at["d", ch] = [
                self.lane.start(self.g.at[ch, mine], self.g.at[ch, mine], device(zz, y, core)) for zz in zs
            ]

        def e(self, ch):
            self.wait("d", ch)
            block = self.g.at[ch, pl.ds((core * yn_count + y) * zn, zn)]
            self.at["e", ch] = [self.lane.start(block, block, device(z, yy, core)) for yy in ys]

        def f(self, ch):
            self.wait("e", ch)
            block = self.g.at[ch, pl.ds(core * half, half)]
            self.at["f", ch] = [self.lane.start(block, block, mate)]

        def h(self, ch):
            self.wait("f", ch)

    def group(ref, ch, gi):
        parts = [ref[ch, gi * subs + s] for s in range(subs)]
        return parts[0] if subs == 1 else jnp.concatenate(parts, axis=1)

    def put_group(ref, ch, gi, value):
        for s in range(subs):
            ref[ch, gi * subs + s] = value[:, s * pcc:(s + 1) * pcc]

    one = Reduce(x1, g1, ra1, rb1, rc1, Lane(send1, recv1))
    two = Reduce(x2, g2, ra2, rb2, rc2, Lane(send2, recv2))
    tiny = Lane(send3, recv3)

    weight = 1.0 / jnp.full((8, LANES), var_ref[0], jnp.float32)
    mask = jnp.full((8, LANES), mask_ref[0, 0].astype(jnp.float32), jnp.float32)
    block_term = weight * mask
    term = block_term[0:1, 0:1]
    lane = lax.broadcasted_iota(jnp.int32, (8, LANES), 1)
    small = jnp.where(lane == TILES, block_term, 0.0)
    for t in range(TILES):
        value = jnp.where(owner_ref[t] == me, zp_ref[0], 0.0)
        small = small + jnp.where(lane == t, value, 0.0)
    s_own[...] = small
    for ch in range(chunks):
        for gi in range(groups):
            put_group(x1, ch, gi, image_ref[0, gi * pr:(gi + 1) * pr, ch * cw:(ch + 1) * cw] * term)

    pl.semaphore_wait(barrier, len(peers))
    tiny_a = [tiny.start(s_own, sa, mate)]
    for ch in range(chunks):
        one.a(ch)

    sharp = image_ref[0].astype(jnp.bfloat16)
    ntile = width // LANES
    zero = jnp.zeros((height, LANES), jnp.bfloat16)
    for t in range(ntile):
        for s in range(3):
            src = t + s - 1
            value = sharp[:, src * LANES:(src + 1) * LANES] if 0 <= src < ntile else zero
            lhs[t * height:(t + 1) * height, s * LANES:(s + 1) * LANES] = value
    off_h = (
        lax.broadcasted_iota(jnp.int32, (3 * LANES, LANES), 0)
        - LANES
        - lax.broadcasted_iota(jnp.int32, (3 * LANES, LANES), 1)
    ).astype(jnp.float32)
    off_v = (
        lax.broadcasted_iota(jnp.int32, (height, height), 1) - lax.broadcasted_iota(jnp.int32, (height, height), 0)
    ).astype(jnp.float32)

    def horizontal(si):
        sigma = sigma_list[si]
        band = jnp.concatenate([tap_values(off_h, sigma, degree) for degree in (0, 1, 2)], axis=1)
        for t in range(0, ntile, 2):
            res = jnp.dot(
                lhs[t * height:(t + 2) * height, :], band, preferred_element_type=jnp.float32
            ).astype(jnp.bfloat16)
            for u in range(2):
                for degree in (0, 1, 2):
                    across[si * 3 + degree, :, (t + u) * LANES:(t + u + 1) * LANES] = res[
                        u * height:(u + 1) * height, degree * LANES:(degree + 1) * LANES
                    ]

    def vertical(si):
        sigma = sigma_list[si]
        bands = [tap_values(off_v, sigma, degree) for degree in (0, 1, 2)]
        for i, j in basis_pairs:
            k = si * 4 + basis_pairs.index((i, j))
            bases[k * height:(k + 1) * height, :] = jnp.dot(
                bands[j], across[si * 3 + i], preferred_element_type=jnp.float32
            ).astype(jnp.bfloat16)

    for si in range(3):
        horizontal(si)

    tiny_a[0].wait_recv()
    s_mid[...] = s_own[...] + sa[...]
    tiny_b = [tiny.start(s_mid, sb.at[d], device(z, yy, core)) for d, yy in enumerate(ys)]
    for ch in range(chunks):
        one.b(ch)

    for si in range(3):
        vertical(si)

    for copy in tiny_b:
        copy.wait_recv()
    total = s_mid[...]
    for d in range(yn_count - 1):
        total = total + sb[d]
    s_sum[...] = total
    tiny_c = [tiny.start(s_sum, sc.at[d], device(zz, y, core)) for d, zz in enumerate(zs)]
    for ch in range(chunks):
        one.c(ch)

    stamp = stamp_ref[...]
    shift = width.bit_length() - 1
    rows = lax.shift_right_logical(stamp, shift)
    cols = stamp - lax.shift_left(rows, shift)
    onehot[...] = jnp.where(
        lax.broadcasted_iota(jnp.int32, (width, npix), 0) == cols, 1.0, 0.0
    ).astype(jnp.bfloat16)
    row_hit = lax.broadcasted_iota(jnp.int32, (height, npix), 0) == rows
    design[...] = jnp.zeros_like(design)

    def pick(k):
        got = jnp.dot(
            bases[k * height:(k + 1) * height, :], onehot[...], preferred_element_type=jnp.float32
        )
        design[16 + k:17 + k, :] = jnp.sum(jnp.where(row_hit, got, 0.0), axis=0, keepdims=True)

    for k in range(NBASIS):
        pick(k)
    design[16 + NBASIS:17 + NBASIS, :] = jnp.ones((1, npix), jnp.float32)
    design[17 + NBASIS:18 + NBASIS, :] = 2.0 * (cols.astype(jnp.float32) + 0.5) / width - 1.0
    design[18 + NBASIS:19 + NBASIS, :] = 2.0 * (rows.astype(jnp.float32) + 0.5) / height - 1.0

    for copy in tiny_c:
        copy.wait_recv()
    total = s_sum[...]
    for d in range(zn - 1):
        total = total + sc[d]
    denom = 1.0 + total[:, TILES:TILES + 1]
    col_in = lax.broadcasted_iota(jnp.int32, (pr, pcc), 1) + lax.rem(mine, subs) * pcc

    def make_reference(ch, numer):
        scale = jnp.broadcast_to(total[:1, 0:1], (pr, pcc))
        for t in range(1, TILES):
            scale = jnp.where(
                col_in + ch * cw >= t * (width // TILES), jnp.broadcast_to(total[:1, t:t + 1], (pr, pcc)), scale
            )
        return numer / jnp.broadcast_to(denom[:1], (pr, pcc)) * scale

    for ch in range(chunks):
        one.d(ch, make_reference)

    rowi = lax.broadcasted_iota(jnp.int32, (16, LANES), 0)
    lanei = lax.broadcasted_iota(jnp.int32, (16, LANES), 1)
    normal = lax.dot_general(
        design[16:32, :], design[...], (((1,), (1,)), ((), ())),
        precision=lax.Precision.HIGHEST, preferred_element_type=jnp.float32,
    )
    aug = jnp.where(lanei == rowi + 16, normal + 0.05 * normal, normal)
    aug = jnp.where(lanei == rowi, 1.0, aug)
    aug = jnp.where((rowi == 15) & (lanei == 31), 1.0, aug)
    for k in range(NBASIS + 3):
        row = aug[k:k + 1, :] / aug[k:k + 1, 16 + k:17 + k]
        aug = jnp.where(rowi == k, row, aug - aug[:, 16 + k:17 + k] * row)

    for ch in range(chunks):
        one.e(ch)
    for ch in range(chunks):
        one.f(ch)

    picked = jnp.zeros((1, npix), jnp.float32)
    for ch in range(chunks):
        one.h(ch)
        got = jnp.zeros((height, npix), jnp.float32)
        ref_img = jnp.concatenate([group(g1, ch, gi) for gi in range(groups)], axis=0)
        hi = ref_img.astype(jnp.bfloat16)
        rest = ref_img - hi.astype(jnp.float32)
        mid = rest.astype(jnp.bfloat16)
        low = (rest - mid.astype(jnp.float32)).astype(jnp.bfloat16)
        for part in (hi, mid, low):
            got = got + jnp.dot(part, onehot[ch * cw:(ch + 1) * cw, :], preferred_element_type=jnp.float32)
        picked = picked + jnp.sum(jnp.where(row_hit, got, 0.0), axis=0, keepdims=True)
    rhs = jnp.sum(design[16:32, :] * picked, axis=1, keepdims=True)
    coef = jnp.sum(aug * rhs, axis=0, keepdims=True)
    coef_ref[...] = coef[:, 0:NBASIS + 3]

    mask_one = mask[0:1, 0:1]
    span = 16
    xn = 2.0 * (lax.broadcasted_iota(jnp.int32, (1, width), 1).astype(jnp.float32) + 0.5) / width - 1.0
    across_x = coef[:, NBASIS:NBASIS + 1] + coef[:, NBASIS + 1:NBASIS + 2] * xn
    coefs = [coef[:, k:k + 1] for k in range(NBASIS + 3)]
    for ch in range(chunks):
        cols_ch = slice(ch * cw, (ch + 1) * cw)
        for r0 in range(0, height, span):
            model = jnp.zeros((span, cw), jnp.float32)
            for k in range(NBASIS):
                model = model + coefs[k] * bases[k * height + r0:k * height + r0 + span, cols_ch].astype(jnp.float32)
            ynv = (
                2.0 * ((lax.broadcasted_iota(jnp.int32, (span, 1), 0) + r0).astype(jnp.float32) + 0.5) / height - 1.0
            )
            model = model + across_x[:, cols_ch] + coefs[NBASIS + 2] * ynv
            for q in range(span // pr):
                gi = r0 // pr + q
                diff = mask_one * (model[q * pr:(q + 1) * pr, :] - group(g1, ch, gi))
                diff_s[gi * pr:(gi + 1) * pr, cols_ch] = diff
                put_group(x2, ch, gi, diff * diff)
        two.a(ch)
    for ch in range(chunks):
        two.b(ch)
    for ch in range(chunks):
        two.c(ch)
    for ch in range(chunks):
        two.d(ch, lambda ch, pooled: 1.0 / jnp.sqrt(0.05 + pooled / count))
    for ch in range(chunks):
        two.e(ch)
    for ch in range(chunks):
        two.f(ch)
    for ch in range(chunks):
        two.h(ch)
        for gi in range(groups):
            out_ref[0, gi * pr:(gi + 1) * pr, ch * cw:(ch + 1) * cw] = diff_s[
                gi * pr:(gi + 1) * pr, ch * cw:(ch + 1) * cw
            ] * group(g2, ch, gi)
    for copy in pending:
        copy.wait_send()


def shards(images, variance, zero_point, block_mask, stamps, owners):
    _, height, width = images.shape
    count = lax.axis_size("epoch")
    npix = stamps.shape[1]
    zn, yn_count = grid_of(count)
    half = zn * yn_count
    pr = max(8, height // count)
    subs = count * pr // height
    chunks = CHUNKS
    while chunks > 1 and width // chunks // subs < LANES:
        chunks //= 2
    pcc = width // chunks // subs
    f32 = jnp.float32
    big = pltpu.VMEM((chunks, count, pr, pcc), f32)
    ra = pltpu.VMEM((chunks, half, pr, pcc), f32)
    rb = pltpu.VMEM((chunks, max(1, yn_count - 1), zn, pr, pcc), f32)
    rc = pltpu.VMEM((chunks, max(1, zn - 1), pr, pcc), f32)
    tile = pltpu.VMEM((8, LANES), f32)
    nsem = chunks * 2 * (1 + (yn_count - 1) + (zn - 1))
    nsmall = 1 + (yn_count - 1) + (zn - 1)
    dma = pltpu.SemaphoreType.DMA
    vmem = pl.BlockSpec(memory_space=pltpu.VMEM)
    smem = pl.BlockSpec(memory_space=pltpu.SMEM)
    return pl.pallas_call(
        functools.partial(kernel, count, height, width),
        out_shape=(
            jax.ShapeDtypeStruct(images.shape, f32),
            jax.ShapeDtypeStruct((1, NBASIS + 3), f32),
        ),
        in_specs=[vmem, smem, smem, smem, smem, vmem],
        out_specs=(vmem, vmem),
        scratch_shapes=[
            big, big, big, big, ra, ra, rb, rb, rc, rc,
            tile, tile, tile, tile,
            pltpu.VMEM((max(1, yn_count - 1), 8, LANES), f32),
            pltpu.VMEM((max(1, zn - 1), 8, LANES), f32),
            pltpu.VMEM((width // LANES * height, 3 * LANES), jnp.bfloat16),
            pltpu.VMEM((9, height, width), jnp.bfloat16),
            pltpu.VMEM((NBASIS * height, width), jnp.bfloat16),
            pltpu.VMEM((width, npix), jnp.bfloat16),
            pltpu.VMEM((LANES, npix), f32),
            pltpu.VMEM((height, width), f32),
            dma((nsem,)), dma((nsem,)), dma((nsem,)), dma((nsem,)), dma((nsmall,)), dma((nsmall,)),
        ],
        compiler_params=pltpu.CompilerParams(
            collective_id=0, has_side_effects=True, vmem_limit_bytes=56 * 1024 * 1024
        ),
    )(images, variance, zero_point, block_mask, owners, stamps)


def solution(mesh):
    in_specs = (
        P(("patch", "epoch"), None, None),
        P(("patch", "epoch")),
        P(("patch", "epoch")),
        P(("patch", "epoch"), None),
        P(("patch", "epoch"), None),
        P("patch"),
    )
    out_specs = (P(("patch", "epoch"), None, None), P(("patch", "epoch"), None))
    return jax.shard_map(shards, mesh=mesh, in_specs=in_specs, out_specs=out_specs, check_vma=False)
```

time: 242 us -> 50.9 us (0.21)
  waiting for transfers between devices: 88.2 us -> 0 us
  local copies, waits for them, and re-layouts: 54.6 us -> 2.4 us
  Pallas kernels: 0 us -> 45.7 us
  blocking collectives: 36.3 us -> 0 us
  matrix products: 24.1 us -> 0 us
  other arithmetic: 21.4 us -> 0 us
  between operations: 17.2 us -> 2.58 us
    psum x2 -> x0, waiting for transfers between devices: 88.2 us -> none  [the longest x1 88.2 us: shards(): pooled = lax.psum(diff * diff, 'epoch')]
    gather x16 -> x0, local copies, waits for them, and re-layouts: 51.7 us -> none  [the longest x12 42.2 us: shards(): jnp.take(b.reshape(-1), stamp_row).astype(jnp.float32)]
    pallas_call x0 -> x1, Pallas kernels: none -> 45.7 us  [shards(): pl.pallas_call(functools.partial(kernel, count, height, width), out_shape...]
    unnamed x1 -> x0, blocking collectives: 36.3 us -> none
    dot_general x17 -> x0, matrix products: 23.8 us -> none  [the longest x12 17 us: shards(): jnp.dot(vertical, across[pair[0]], preferred_element_type=jnp.float32)]
    mul x3 -> x0, other arithmetic: 12 us -> none  [the longest x1 10.7 us: shards(): pooled = lax.psum(diff * diff, 'epoch')]
    another operation x6 -> x0, other arithmetic: 3.85 us -> none  [the longest x3 2.04 us: shards(): factor = jnp.linalg.cholesky(normal)]
  transfers between devices with their start and end apart: 2 -> 0, of which waited for: 1 -> 0; matrix products, arithmetic and copies ran while one was open for 30% -> 0% of each run, Pallas kernels for 0% -> 0%
where the time goes in v1:
time: 50.9 us; the launch traced here: 50.7 us
  Pallas kernels  45.7 us (90%)
  between operations  2.58 us (5%)
  local copies, waits for them, and re-layouts  2.4 us (5%)
    pallas_call x1, Pallas kernels, shards(): pl.pallas_call(functools.partial(kernel, count, height, width), out_shape...  45.7 us
    unnamed x4, local copies, waits for them, and re-layouts  2.4 us

profile of v1, /device:TPU:0, one launch (start us, length us, event | category | flops | bytes accessed | tf_op | source)
XLA Modules:
  0.0 50.7 jit_solution(14252304946825947641)
XLA Ops:
  2.6 45.7 %shard_map.77 = (f32[1,128,1024]{2,1,0:T(8,128)}, f32[1,15]{1,0:T(1,128)}) custom-call(f32[1,128,1024]{2,1,0:T(8,128)} %image_ref.1, f32[1]{0:T(128)S(6)} %copy.10.var_ref, f32[1]{0:T(128)S(6)} %copy.11.zp_ref, s32[1,1]{1,0:T(1,128)S(6)} %copy.12.mask_ref, s32[4]{0:T(128)} %owner_ref.1, s32[1,512]{1,0:T(1,128)} %stamp_ref.1), custom_call_target="tpu_custom_call" | custom-call | tf_op jit(solution)/shard_map/pallas_call | solution.py:385
  48.3 0.0 copy-start
  48.3 1.9 %copy.13 = f32[1,128,1024]{2,1,0:T(8,128)} copy(f32[1,128,1024]{2,1,0:T(8,128)} %get-tuple-element.4) | data formatting | bytes 1048576
  50.2 0.0 copy-done
  50.2 0.5 %copy.14 = f32[1,15]{1,0:T(1,128)} copy(f32[1,15]{1,0:T(1,128)S(1)} %copy-done) | data formatting | bytes 120
Async XLA Ops:
  48.3 1.9 %copy-start = (f32[1,15]{1,0:T(1,128)S(1)}, f32[1,15]{1,0:T(1,128)}, u32[]{:S(2)}) copy-start(f32[1,15]{1,0:T(1,128)} %get-tuple-element.5) | copy-start | bytes 184

commit v2 on v1

v2 whole, which is shorter than its diff:
```python
import functools
import math

import jax
import jax.numpy as jnp
from jax import lax
from jax.experimental import pallas as pl
from jax.experimental.pallas import tpu as pltpu
from jax.sharding import PartitionSpec as P

TILES = 4
KHALF = 7
NBASIS = 12
LANES = 128

sigma_list = (0.75, 1.5, 3.0)
basis_pairs = ((0, 0), (2, 0), (0, 2), (1, 1))
MESH = pl.DeviceIdType.MESH


def tap_values(offset, sigma, degree):
    scaled = offset / sigma
    power = jnp.ones_like(scaled)
    for _ in range(degree):
        power = power * scaled
    value = jnp.exp(-0.5 * scaled * scaled) * power / (math.sqrt(2.0 * math.pi) * sigma)
    return jnp.where(jnp.abs(offset) <= KHALF, value, 0.0).astype(jnp.bfloat16)


def grid_of(count):
    chips = count // 2
    middle = 1
    while middle * 2 * middle * 2 <= chips:
        middle *= 2
    if chips % middle:
        middle = 1
    return chips // middle, middle


def kernel(
    count, height, width,
    image_ref, var_ref, zp_ref, mask_ref, owner_ref, stamp_ref,
    diff_ref, inv_ref, coef_ref,
    x1, x2, g1, g2, ra1, ra2, rb1, rb2, rc1, rc2,
    s_own, s_mid, s_sum, sa, sb, sc,
    lhs, across, bases, onehot, design,
    send1, recv1, send2, recv2, send3, recv3,
):
    zn, yn_count = grid_of(count)
    half = zn * yn_count
    _, pr, pcc = x1.shape
    subs = width // pcc
    groups = height // pr
    npix = stamp_ref.shape[1]

    me = lax.axis_index("epoch")
    core = lax.rem(me, 2)
    chip = me // 2
    y = lax.rem(chip, yn_count)
    z = chip // yn_count

    def device(zz, yy, cc):
        return {"epoch": (zz * yn_count + yy) * 2 + cc}

    def flip(value, m):
        bit = 1
        while bit <= m:
            if m & bit:
                value = value + bit * (1 - 2 * lax.rem(value // bit, 2))
            bit *= 2
        return value

    mate = device(z, y, 1 - core)
    ys = [flip(y, e) for e in range(1, yn_count)]
    zs = [flip(z, m) for m in range(1, zn)]
    peers = [mate] + [device(z, yy, core) for yy in ys] + [device(zz, y, core) for zz in zs]
    mine = (core * yn_count + y) * zn + z

    barrier = pltpu.get_barrier_semaphore()
    for peer in peers:
        pl.semaphore_signal(barrier, inc=1, device_id=peer, device_id_type=MESH)

    pending = []

    class Lane:
        def __init__(self, send, recv):
            self.send, self.recv, self.next = send, recv, 0

        def start(self, src, dst, device_id):
            copy = pltpu.make_async_remote_copy(
                src_ref=src, dst_ref=dst, send_sem=self.send.at[self.next], recv_sem=self.recv.at[self.next],
                device_id=device_id, device_id_type=MESH,
            )
            self.next += 1
            copy.start()
            pending.append(copy)
            return copy

    order = list(range(zn - 1, -1, -1))

    class Reduce:
        def __init__(self, x, g, ra, rb, rc, lane):
            self.x, self.g, self.ra, self.rb, self.rc, self.lane = x, g, ra, rb, rc, lane
            self.at = {}

        def a(self):
            for m in order:
                zz = flip(z, m)
                for e in list(range(1, yn_count)) + [0]:
                    src = flip(y, e) * zn + zz
                    self.at["a", e, m] = self.lane.start(
                        self.x.at[(1 - core) * half + src], self.ra.at[src], mate
                    )

        def b(self, m):
            zz = flip(z, m)
            for e in range(1, yn_count):
                yy = flip(y, e)
                own = core * half + yy * zn + zz
                self.at["a", e, m].wait_recv()
                self.x[own] = self.x[own] + self.ra[yy * zn + zz]
                self.at["b", e, m] = self.lane.start(self.x.at[own], self.rb.at[e - 1, zz], device(z, yy, core))

        def c(self, m):
            zz = flip(z, m)
            own = core * half + y * zn + zz
            self.at["a", 0, m].wait_recv()
            total = self.x[own] + self.ra[y * zn + zz]
            for e in range(1, yn_count):
                self.at["b", e, m].wait_recv()
                total = total + self.rb[e - 1, zz]
            self.x[own] = total
            if m:
                self.at["c", m] = self.lane.start(self.x.at[own], self.rc.at[m - 1], device(zz, y, core))

        def d(self, final):
            total = self.x[mine]
            for m in order[::-1]:
                if m:
                    self.at["c", m].wait_recv()
                    total = total + self.rc[m - 1]
            self.g[mine] = final(total)
            for m in order:
                if m:
                    self.at["d", m] = self.lane.start(
                        self.g.at[mine], self.g.at[mine], device(flip(z, m), y, core)
                    )
            self.forward(0)

        def forward(self, m):
            if m:
                self.at["d", m].wait_recv()
            block = self.g.at[(core * yn_count + y) * zn + flip(z, m)]
            for e in range(1, yn_count):
                self.at["e", e, m] = self.lane.start(block, block, device(z, flip(y, e), core))
            self.at["f", 0, m] = self.lane.start(block, block, mate)

        def mate_on(self, m):
            for e in range(1, yn_count):
                self.at["e", e, m].wait_recv()
                block = self.g.at[(core * yn_count + flip(y, e)) * zn + flip(z, m)]
                self.at["f", e, m] = self.lane.start(block, block, mate)

        def end(self):
            for m in order[::-1]:
                for e in range(yn_count):
                    self.at["f", e, m].wait_recv()

    def group(ref, gi):
        parts = [ref[gi * subs + s] for s in range(subs)]
        return parts[0] if subs == 1 else jnp.concatenate(parts, axis=1)

    def put_group(ref, gi, value):
        for s in range(subs):
            ref[gi * subs + s] = value[:, s * pcc:(s + 1) * pcc]

    one = Reduce(x1, g1, ra1, rb1, rc1, Lane(send1, recv1))
    two = Reduce(x2, g2, ra2, rb2, rc2, Lane(send2, recv2))
    tiny = Lane(send3, recv3)

    weight = 1.0 / jnp.broadcast_to(var_ref[...], (8, LANES))
    mask = jnp.broadcast_to(mask_ref[...].astype(jnp.float32), (8, LANES))
    block_term = weight * mask
    term = block_term[0:1, 0:1]
    lane = lax.broadcasted_iota(jnp.int32, (8, LANES), 1)
    small = jnp.where(lane == TILES, block_term, 0.0)
    for t in range(TILES):
        owned = jnp.broadcast_to(owner_ref[:, t:t + 1], (8, LANES)) == me
        small = small + jnp.where((lane == t) & owned, jnp.broadcast_to(zp_ref[...], (8, LANES)), 0.0)
    s_own[...] = small
    for gi in range(groups):
        put_group(x1, gi, image_ref[0, gi * pr:(gi + 1) * pr, :] * term)

    pl.semaphore_wait(barrier, len(peers))
    tiny_a = [tiny.start(s_own, sa, mate)]
    one.a()

    sharp = image_ref[0].astype(jnp.bfloat16)
    ntile = width // LANES
    zero = jnp.zeros((height, LANES), jnp.bfloat16)
    for t in range(ntile):
        for s in range(3):
            src = t + s - 1
            value = sharp[:, src * LANES:(src + 1) * LANES] if 0 <= src < ntile else zero
            lhs[t * height:(t + 1) * height, s * LANES:(s + 1) * LANES] = value
    off_h = (
        lax.broadcasted_iota(jnp.int32, (3 * LANES, LANES), 0)
        - LANES
        - lax.broadcasted_iota(jnp.int32, (3 * LANES, LANES), 1)
    ).astype(jnp.float32)
    off_v = (
        lax.broadcasted_iota(jnp.int32, (height, height), 1) - lax.broadcasted_iota(jnp.int32, (height, height), 0)
    ).astype(jnp.float32)

    def horizontal(si):
        sigma = sigma_list[si]
        band = jnp.concatenate([tap_values(off_h, sigma, degree) for degree in (0, 1, 2)], axis=1)
        for t in range(0, ntile, 2):
            res = jnp.dot(
                lhs[t * height:(t + 2) * height, :], band, preferred_element_type=jnp.float32
            ).astype(jnp.bfloat16)
            for u in range(2):
                for degree in (0, 1, 2):
                    across[si * 3 + degree, :, (t + u) * LANES:(t + u + 1) * LANES] = res[
                        u * height:(u + 1) * height, degree * LANES:(degree + 1) * LANES
                    ]

    def vertical(si):
        sigma = sigma_list[si]
        bands = [tap_values(off_v, sigma, degree) for degree in (0, 1, 2)]
        for i, j in basis_pairs:
            k = si * 4 + basis_pairs.index((i, j))
            bases[k * height:(k + 1) * height, :] = jnp.dot(
                bands[j], across[si * 3 + i], preferred_element_type=jnp.float32
            ).astype(jnp.bfloat16)

    horizontal(0)

    tiny_a[0].wait_recv()
    s_mid[...] = s_own[...] + sa[...]
    tiny_b = [tiny.start(s_mid, sb.at[d], device(z, yy, core)) for d, yy in enumerate(ys)]
    for m in order:
        one.b(m)

    horizontal(1)

    for copy in tiny_b:
        copy.wait_recv()
    total = s_mid[...]
    for d in range(yn_count - 1):
        total = total + sb[d]
    s_sum[...] = total
    tiny_c = [tiny.start(s_sum, sc.at[d], device(zz, y, core)) for d, zz in enumerate(zs)]
    for m in order:
        one.c(m)
    horizontal(2)
    for si in range(3):
        vertical(si)

    stamp = stamp_ref[...]
    shift = width.bit_length() - 1
    rows = lax.shift_right_logical(stamp, shift)
    cols = stamp - lax.shift_left(rows, shift)
    onehot[...] = jnp.where(
        lax.broadcasted_iota(jnp.int32, (width, npix), 0) == cols, 1.0, 0.0
    ).astype(jnp.bfloat16)
    row_hit = lax.broadcasted_iota(jnp.int32, (height, npix), 0) == rows
    design[...] = jnp.zeros_like(design)

    def pick(k):
        got = jnp.dot(
            bases[k * height:(k + 1) * height, :], onehot[...], preferred_element_type=jnp.float32
        )
        design[16 + k:17 + k, :] = jnp.sum(jnp.where(row_hit, got, 0.0), axis=0, keepdims=True)

    design[16 + NBASIS:17 + NBASIS, :] = jnp.ones((1, npix), jnp.float32)
    design[17 + NBASIS:18 + NBASIS, :] = 2.0 * (cols.astype(jnp.float32) + 0.5) / width - 1.0
    design[18 + NBASIS:19 + NBASIS, :] = 2.0 * (rows.astype(jnp.float32) + 0.5) / height - 1.0

    for copy in tiny_c:
        copy.wait_recv()
    total = s_sum[...]
    for d in range(zn - 1):
        total = total + sc[d]
    denom = 1.0 + total[:, TILES:TILES + 1]
    col_in = lax.broadcasted_iota(jnp.int32, (pr, pcc), 1) + lax.rem(mine, subs) * pcc

    def make_reference(numer):
        scale = jnp.broadcast_to(total[:1, 0:1], (pr, pcc))
        for t in range(1, TILES):
            scale = jnp.where(
                col_in >= t * (width // TILES), jnp.broadcast_to(total[:1, t:t + 1], (pr, pcc)), scale
            )
        return numer / jnp.broadcast_to(denom[:1], (pr, pcc)) * scale

    one.d(make_reference)
    for k in range(NBASIS // 2):
        pick(k)
    for m in range(1, zn):
        one.forward(m)
    for k in range(NBASIS // 2, NBASIS):
        pick(k)
    for m in range(zn):
        one.mate_on(m)

    rowi = lax.broadcasted_iota(jnp.int32, (16, LANES), 0)
    lanei = lax.broadcasted_iota(jnp.int32, (16, LANES), 1)
    normal = lax.dot_general(
        design[16:32, :], design[...], (((1,), (1,)), ((), ())),
        precision=lax.Precision.HIGHEST, preferred_element_type=jnp.float32,
    )
    aug = jnp.where(lanei == rowi + 16, normal + 0.05 * normal, normal)
    aug = jnp.where(lanei == rowi, 1.0, aug)
    aug = jnp.where((rowi == 15) & (lanei == 31), 1.0, aug)
    for k in range(NBASIS + 3):
        row = aug[k:k + 1, :] / aug[k:k + 1, 16 + k:17 + k]
        aug = jnp.where(rowi == k, row, aug - aug[:, 16 + k:17 + k] * row)

    one.end()
    ref_img = jnp.concatenate([group(g1, gi) for gi in range(groups)], axis=0)
    hi = ref_img.astype(jnp.bfloat16)
    rest = ref_img - hi.astype(jnp.float32)
    mid = rest.astype(jnp.bfloat16)
    low = (rest - mid.astype(jnp.float32)).astype(jnp.bfloat16)
    got = jnp.zeros((height, npix), jnp.float32)
    for part in (hi, mid, low):
        got = got + jnp.dot(part, onehot[...], preferred_element_type=jnp.float32)
    picked = jnp.sum(jnp.where(row_hit, got, 0.0), axis=0, keepdims=True)
    rhs = jnp.sum(design[16:32, :] * picked, axis=1, keepdims=True)
    coef = jnp.sum(aug * rhs, axis=0, keepdims=True)
    coef_ref[...] = coef[:, 0:NBASIS + 3]

    mask_one = mask[0:1, 0:1]
    span = 16
    xn = 2.0 * (lax.broadcasted_iota(jnp.int32, (1, width), 1).astype(jnp.float32) + 0.5) / width - 1.0
    across_x = coef[:, NBASIS:NBASIS + 1] + coef[:, NBASIS + 1:NBASIS + 2] * xn
    coefs = [coef[:, k:k + 1] for k in range(NBASIS + 3)]
    for r0 in range(0, height, span):
        model = jnp.zeros((span, width), jnp.float32)
        for k in range(NBASIS):
            model = model + coefs[k] * bases[k * height + r0:k * height + r0 + span, :].astype(jnp.float32)
        ynv = 2.0 * ((lax.broadcasted_iota(jnp.int32, (span, 1), 0) + r0).astype(jnp.float32) + 0.5) / height - 1.0
        model = model + across_x + coefs[NBASIS + 2] * ynv
        for q in range(span // pr):
            gi = r0 // pr + q
            diff = mask_one * (model[q * pr:(q + 1) * pr, :] - group(g1, gi))
            diff_ref[gi * pr:(gi + 1) * pr, :] = diff
            put_group(x2, gi, diff * diff)
    two.a()
    for m in order:
        two.b(m)
    for m in order:
        two.c(m)
    two.d(lambda pooled: 1.0 / jnp.sqrt(0.05 + pooled / count))
    for m in range(1, zn):
        two.forward(m)
    for m in range(zn):
        two.mate_on(m)
    two.end()
    for gi in range(groups):
        inv_ref[gi * pr:(gi + 1) * pr, :] = group(g2, gi)
    for copy in pending:
        copy.wait_send()


def finish(diff_ref, inv_ref, coef_in, out_ref, coef_ref):
    out_ref[0] = diff_ref[...] * inv_ref[...]
    coef_ref[...] = coef_in[...]


def shards(images, variance, zero_point, block_mask, stamps, owners):
    _, height, width = images.shape
    count = lax.axis_size("epoch")
    npix = stamps.shape[1]
    zn, yn_count = grid_of(count)
    half = zn * yn_count
    pr = max(8, height // count)
    subs = count * pr // height
    pcc = width // subs
    f32 = jnp.float32
    big = pltpu.VMEM((count, pr, pcc), f32)
    ra = pltpu.VMEM((half, pr, pcc), f32)
    rb = pltpu.VMEM((max(1, yn_count - 1), zn, pr, pcc), f32)
    rc = pltpu.VMEM((max(1, zn - 1), pr, pcc), f32)
    tile = pltpu.VMEM((8, LANES), f32)
    nsem = 2 * (half + (yn_count - 1) * zn + (zn - 1))
    nsmall = 1 + (yn_count - 1) + (zn - 1)
    dma = pltpu.SemaphoreType.DMA
    vmem = pl.BlockSpec(memory_space=pltpu.VMEM)
    diff, inv, coef = pl.pallas_call(
        functools.partial(kernel, count, height, width),
        out_shape=(
            jax.ShapeDtypeStruct((height, width), f32),
            jax.ShapeDtypeStruct((height, width), f32),
            jax.ShapeDtypeStruct((1, NBASIS + 3), f32),
        ),
        in_specs=[vmem] * 6,
        out_specs=(vmem,) * 3,
        scratch_shapes=[
            big, big, big, big, ra, ra, rb, rb, rc, rc,
            tile, tile, tile, tile,
            pltpu.VMEM((max(1, yn_count - 1), 8, LANES), f32),
            pltpu.VMEM((max(1, zn - 1), 8, LANES), f32),
            pltpu.VMEM((width // LANES * height, 3 * LANES), jnp.bfloat16),
            pltpu.VMEM((9, height, width), jnp.bfloat16),
            pltpu.VMEM((NBASIS * height, width), jnp.bfloat16),
            pltpu.VMEM((width, npix), jnp.bfloat16),
            pltpu.VMEM((LANES, npix), f32),
            dma((nsem,)), dma((nsem,)), dma((nsem,)), dma((nsem,)), dma((nsmall,)), dma((nsmall,)),
        ],
        compiler_params=pltpu.CompilerParams(
            collective_id=0, has_side_effects=True, vmem_limit_bytes=40 * 1024 * 1024
        ),
    )(
        images, variance.reshape(1, 1), zero_point.reshape(1, 1), block_mask, owners.reshape(1, -1), stamps
    )
    return pl.pallas_call(
        finish,
        out_shape=(
            jax.ShapeDtypeStruct(images.shape, f32),
            jax.ShapeDtypeStruct((1, NBASIS + 3), f32),
        ),
        in_specs=[vmem] * 3,
        out_specs=(vmem,) * 2,
        compiler_params=pltpu.CompilerParams(vmem_limit_bytes=8 * 1024 * 1024),
    )(diff, inv, coef)


def solution(mesh):
    in_specs = (
        P(("patch", "epoch"), None, None),
        P(("patch", "epoch")),
        P(("patch", "epoch")),
        P(("patch", "epoch"), None),
        P(("patch", "epoch"), None),
        P("patch"),
    )
    out_specs = (P(("patch", "epoch"), None, None), P(("patch", "epoch"), None))
    return jax.shard_map(shards, mesh=mesh, in_specs=in_specs, out_specs=out_specs, check_vma=False)
```

time: 50.9 us -> 48.7 us (0.957)
  Pallas kernels: 45.7 us -> 44.2 us
  local copies, waits for them, and re-layouts: 2.4 us -> 1.71 us
    pallas_call x1, Pallas kernels: 45.7 us -> 43.3 us  [shards(): pl.pallas_call(functools.partial(kernel, count, height, width), out_shape...]
    pallas_call x0 -> x1, Pallas kernels: none -> 0.85 us  [shards(): pl.pallas_call(finish, out_shape=(jax.ShapeDtypeStruct(images.shape, f32)...]
    unnamed x4 -> x6, local copies, waits for them, and re-layouts: 2.4 us -> 1.71 us
where the time goes in v2:
time: 48.7 us; the launch traced here: 48.5 us
  Pallas kernels  44.2 us (91%)
  between operations  2.59 us (5%)
  local copies, waits for them, and re-layouts  1.71 us (4%)
    pallas_call x1, Pallas kernels, shards(): pl.pallas_call(functools.partial(kernel, count, height, width), out_shape...  43.3 us
    unnamed x6, local copies, waits for them, and re-layouts  1.71 us

profile of v2, /device:TPU:0, one launch (start us, length us, event | category | flops | bytes accessed | tf_op | source)
XLA Modules:
  0.0 48.5 jit_solution(5183177111663075339)
XLA Ops:
  2.6 0.0 copy-start.1
  2.6 0.0 copy-start.2
  2.6 0.7 %copy-done.1 = s32[1,512]{1,0:T(1,128)S(1)} copy-done((s32[1,512]{1,0:T(1,128)S(1)}, s32[1,512]{1,0:T(1,128)}, u32[]{:S(2)}) %copy-start.1) | copy-done | bytes 2072
  3.2 0.0 copy-done.2
  3.3 0.0 copy-start
  3.3 1.0 %copy-done = f32[1,128,1024]{2,1,0:T(8,128)S(1)} copy-done((f32[1,128,1024]{2,1,0:T(8,128)S(1)}, f32[1,128,1024]{2,1,0:T(8,128)}, u32[]{:S(2)}) %copy-start) | copy-done | bytes 524312
  4.3 43.3 %shard_map.77 = (f32[128,1024]{1,0:T(8,128)S(1)}, f32[128,1024]{1,0:T(8,128)S(1)}, f32[1,15]{1,0:T(1,128)S(1)}) custom-call(f32[1,128,1024]{2,1,0:T(8,128)S(1)} %copy-done, f32[1,1]{1,0:T(1,128)} %bitcast.3.var_ref, f32[1,1]{1,0:T(1,128)} %bitcast.4.zp_ref, s32[1,1]{1,0:T(1,128)S(6)} %copy.10.mask_ref, s32[1,4]{1,0:T(1,128)S(1)} %bitcast.5, ...), custom_call_target="tpu_custom_call" | custom-call | tf_op jit(solution)/shard_map/pallas_call | solution.py:390
  47.6 0.9 %shard_map.78 = (f32[1,128,1024]{2,1,0:T(8,128)}, f32[1,15]{1,0:T(1,128)}) custom-call(f32[128,1024]{1,0:T(8,128)S(1)} %get-tuple-element.5.diff_ref, f32[128,1024]{1,0:T(8,128)S(1)} %get-tuple-element.6.inv_ref, f32[1,15]{1,0:T(1,128)S(1)} %get-tuple-element.7.coef_in), custom_call_target="tpu_custom_call" | custom-call | tf_op jit(solution)/shard_map/pallas_call | solution.py:417
Async XLA Ops:
  2.6 0.7 %copy-start.1 = (s32[1,512]{1,0:T(1,128)S(1)}, s32[1,512]{1,0:T(1,128)}, u32[]{:S(2)}) copy-start(s32[1,512]{1,0:T(1,128)} %stamp_ref.1) | copy-start | bytes 6148
  2.6 0.7 %copy-start.2 = (s32[4]{0:T(128)S(1)}, s32[4]{0:T(128)}, u32[]{:S(2)}) copy-start(s32[4]{0:T(128)} %param.11) | copy-start | bytes 52
  3.3 1.0 %copy-start = (f32[1,128,1024]{2,1,0:T(8,128)S(1)}, f32[1,128,1024]{2,1,0:T(8,128)}, u32[]{:S(2)}) copy-start(f32[1,128,1024]{2,1,0:T(8,128)} %image_ref.1) | copy-start | bytes 1572868

commit v3 on v2

--- a/solution.py
+++ b/solution.py
@@ -39,11 +39,12 @@
 
 def kernel(
     count, height, width,
-    image_ref, var_ref, zp_ref, mask_ref, owner_ref, stamp_ref,
+    image_in, var_in, zp_in, mask_in, owner_in, stamp_in,
     diff_ref, inv_ref, coef_ref,
     x1, x2, g1, g2, ra1, ra2, rb1, rb2, rc1, rc2,
     s_own, s_mid, s_sum, sa, sb, sc,
     lhs, across, bases, onehot, design,
+    image_ref, var_ref, zp_ref, mask_ref, owner_ref, stamp_ref, load,
     send1, recv1, send2, recv2, send3, recv3,
 ):
     zn, yn_count = grid_of(count)
@@ -79,6 +80,16 @@
     barrier = pltpu.get_barrier_semaphore()
     for peer in peers:
         pl.semaphore_signal(barrier, inc=1, device_id=peer, device_id_type=MESH)
+
+    loads = [
+        pltpu.make_async_copy(src, dst, load.at[i])
+        for i, (src, dst) in enumerate((
+            (image_in, image_ref), (var_in, var_ref), (mask_in, mask_ref),
+            (zp_in, zp_ref), (owner_in, owner_ref), (stamp_in, stamp_ref),
+        ))
+    ]
+    for copy in loads:
+        copy.start()
 
     pending = []
 
@@ -178,15 +189,17 @@
     two = Reduce(x2, g2, ra2, rb2, rc2, Lane(send2, recv2))
     tiny = Lane(send3, recv3)
 
-    weight = 1.0 / jnp.broadcast_to(var_ref[...], (8, LANES))
-    mask = jnp.broadcast_to(mask_ref[...].astype(jnp.float32), (8, LANES))
+    for copy in loads:
+        copy.wait()
+    weight = 1.0 / jnp.full((8, LANES), var_ref[0], jnp.float32)
+    mask = jnp.full((8, LANES), mask_ref[0, 0].astype(jnp.float32), jnp.float32)
     block_term = weight * mask
     term = block_term[0:1, 0:1]
     lane = lax.broadcasted_iota(jnp.int32, (8, LANES), 1)
     small = jnp.where(lane == TILES, block_term, 0.0)
     for t in range(TILES):
-        owned = jnp.broadcast_to(owner_ref[:, t:t + 1], (8, LANES)) == me
-        small = small + jnp.where((lane == t) & owned, jnp.broadcast_to(zp_ref[...], (8, LANES)), 0.0)
+        value = jnp.where(owner_ref[t] == me, zp_ref[0], 0.0)
+        small = small + jnp.where(lane == t, value, 0.0)
     s_own[...] = small
     for gi in range(groups):
         put_group(x1, gi, image_ref[0, gi * pr:(gi + 1) * pr, :] * term)
@@ -316,16 +329,23 @@
         row = aug[k:k + 1, :] / aug[k:k + 1, 16 + k:17 + k]
         aug = jnp.where(rowi == k, row, aug - aug[:, 16 + k:17 + k] * row)
 
+    mid_row = height // 2
+    half_row = lax.broadcasted_iota(jnp.int32, (mid_row, npix), 0)
+
+    def picked_of(side):
+        ref_img = jnp.concatenate([group(g1, side * (groups // 2) + gi) for gi in range(groups // 2)], axis=0)
+        hi = ref_img.astype(jnp.bfloat16)
+        rest = ref_img - hi.astype(jnp.float32)
+        mid = rest.astype(jnp.bfloat16)
+        low = (rest - mid.astype(jnp.float32)).astype(jnp.bfloat16)
+        got = jnp.zeros((mid_row, npix), jnp.float32)
+        for part in (hi, mid, low):
+            got = got + jnp.dot(part, onehot[...], preferred_element_type=jnp.float32)
+        return jnp.sum(jnp.where(half_row + side * mid_row == rows, got, 0.0), axis=0, keepdims=True)
+
+    picked = picked_of(core)
     one.end()
-    ref_img = jnp.concatenate([group(g1, gi) for gi in range(groups)], axis=0)
-    hi = ref_img.astype(jnp.bfloat16)
-    rest = ref_img - hi.astype(jnp.float32)
-    mid = rest.astype(jnp.bfloat16)
-    low = (rest - mid.astype(jnp.float32)).astype(jnp.bfloat16)
-    got = jnp.zeros((height, npix), jnp.float32)
-    for part in (hi, mid, low):
-        got = got + jnp.dot(part, onehot[...], preferred_element_type=jnp.float32)
-    picked = jnp.sum(jnp.where(row_hit, got, 0.0), axis=0, keepdims=True)
+    picked = picked + picked_of(1 - core)
     rhs = jnp.sum(design[16:32, :] * picked, axis=1, keepdims=True)
     coef = jnp.sum(aug * rhs, axis=0, keepdims=True)
     coef_ref[...] = coef[:, 0:NBASIS + 3]
@@ -336,17 +356,20 @@
     across_x = coef[:, NBASIS:NBASIS + 1] + coef[:, NBASIS + 1:NBASIS + 2] * xn
     coefs = [coef[:, k:k + 1] for k in range(NBASIS + 3)]
     for r0 in range(0, height, span):
+        side = 1 - core if r0 < mid_row else core
+        if r0 == mid_row:
+            two.a()
+        row = pl.multiple_of(side * mid_row + r0 % mid_row, span)
         model = jnp.zeros((span, width), jnp.float32)
         for k in range(NBASIS):
-            model = model + coefs[k] * bases[k * height + r0:k * height + r0 + span, :].astype(jnp.float32)
-        ynv = 2.0 * ((lax.broadcasted_iota(jnp.int32, (span, 1), 0) + r0).astype(jnp.float32) + 0.5) / height - 1.0
+            model = model + coefs[k] * bases[pl.ds(k * height + row, span), :].astype(jnp.float32)
+        ynv = 2.0 * ((lax.broadcasted_iota(jnp.int32, (span, 1), 0) + row).astype(jnp.float32) + 0.5) / height - 1.0
         model = model + across_x + coefs[NBASIS + 2] * ynv
         for q in range(span // pr):
-            gi = r0 // pr + q
+            gi = row // pr + q
             diff = mask_one * (model[q * pr:(q + 1) * pr, :] - group(g1, gi))
-            diff_ref[gi * pr:(gi + 1) * pr, :] = diff
+            diff_ref[pl.ds(pl.multiple_of(row + q * pr, pr), pr), :] = diff
             put_group(x2, gi, diff * diff)
-    two.a()
     for m in order:
         two.b(m)
     for m in order:
@@ -394,7 +417,7 @@
             jax.ShapeDtypeStruct((height, width), f32),
             jax.ShapeDtypeStruct((1, NBASIS + 3), f32),
         ),
-        in_specs=[vmem] * 6,
+        in_specs=[pl.BlockSpec(memory_space=pltpu.HBM)] * 6,
         out_specs=(vmem,) * 3,
         scratch_shapes=[
             big, big, big, big, ra, ra, rb, rb, rc, rc,
@@ -406,14 +429,16 @@
             pltpu.VMEM((NBASIS * height, width), jnp.bfloat16),
             pltpu.VMEM((width, npix), jnp.bfloat16),
             pltpu.VMEM((LANES, npix), f32),
+            pltpu.VMEM(images.shape, f32),
+            pltpu.SMEM((1,), f32), pltpu.SMEM((1,), f32),
+            pltpu.SMEM(block_mask.shape, jnp.int32), pltpu.SMEM(owners.shape, jnp.int32),
+            pltpu.VMEM(stamps.shape, jnp.int32), dma((6,)),
             dma((nsem,)), dma((nsem,)), dma((nsem,)), dma((nsem,)), dma((nsmall,)), dma((nsmall,)),
         ],
         compiler_params=pltpu.CompilerParams(
             collective_id=0, has_side_effects=True, vmem_limit_bytes=40 * 1024 * 1024
         ),
-    )(
-        images, variance.reshape(1, 1), zero_point.reshape(1, 1), block_mask, owners.reshape(1, -1), stamps
-    )
+    )(images, variance, zero_point, block_mask, owners, stamps)
     return pl.pallas_call(
         finish,
         out_shape=(

time: 48.7 us -> 47.7 us (0.979)
  local copies, waits for them, and re-layouts: 1.71 us -> 1.04 us
    unnamed x6, local copies, waits for them, and re-layouts: 1.71 us -> 1.04 us
where the time goes in v3:
time: 47.7 us; the launch traced here: 47.5 us
  Pallas kernels  43.9 us (92%)
  between operations  2.64 us (6%)
  local copies, waits for them, and re-layouts  1.04 us (2%)
    pallas_call x1, Pallas kernels, shards(): pl.pallas_call(functools.partial(kernel, count, height, width), out_shape...  43 us
    unnamed x6, local copies, waits for them, and re-layouts  1.04 us

profile of v3, /device:TPU:0, one launch (start us, length us, event | category | flops | bytes accessed | tf_op | source)
XLA Modules:
  0.0 47.5 jit_solution(16042504168075938874)
XLA Ops:
  1.3 0.0 copy-start.1
  1.9 0.0 copy-start.2
  2.6 0.0 copy-done.1
  2.6 0.0 copy-done.2
  2.6 0.0 copy-start
  2.6 1.0 %copy-done = f32[1,128,1024]{2,1,0:T(8,128)S(1)} copy-done((f32[1,128,1024]{2,1,0:T(8,128)S(1)}, f32[1,128,1024]{2,1,0:T(8,128)}, u32[]{:S(2)}) %copy-start) | copy-done | bytes 524312
  3.7 43.0 %shard_map.77 = (f32[128,1024]{1,0:T(8,128)S(1)}, f32[128,1024]{1,0:T(8,128)S(1)}, f32[1,15]{1,0:T(1,128)S(1)}) custom-call(f32[1,128,1024]{2,1,0:T(8,128)S(1)} %copy-done, f32[1]{0:T(128)S(6)} %copy.8.var_in, f32[1]{0:T(128)S(6)} %copy.9.zp_in, s32[1,1]{1,0:T(1,128)S(6)} %copy.10.mask_in, s32[4]{0:T(128)S(1)} %copy-done.2, s32[1,512]{1,0:T(1,128)S(1)} %copy-done.1), custom_call_target="tpu_custom_call" | custom-call | tf_op jit(solution)/shard_map/pallas_call | solution.py:413
  46.7 0.9 %shard_map.78 = (f32[1,128,1024]{2,1,0:T(8,128)}, f32[1,15]{1,0:T(1,128)}) custom-call(f32[128,1024]{1,0:T(8,128)S(1)} %get-tuple-element.5.diff_ref, f32[128,1024]{1,0:T(8,128)S(1)} %get-tuple-element.6.inv_ref, f32[1,15]{1,0:T(1,128)S(1)} %get-tuple-element.7.coef_in), custom_call_target="tpu_custom_call" | custom-call | tf_op jit(solution)/shard_map/pallas_call | solution.py:442
Async XLA Ops:
  1.3 1.3 %copy-start.1 = (s32[1,512]{1,0:T(1,128)S(1)}, s32[1,512]{1,0:T(1,128)}, u32[]{:S(2)}) copy-start(s32[1,512]{1,0:T(1,128)} %stamp_in.1) | copy-start | bytes 6148
  1.9 0.7 %copy-start.2 = (s32[4]{0:T(128)S(1)}, s32[4]{0:T(128)}, u32[]{:S(2)}) copy-start(s32[4]{0:T(128)} %owner_in.1) | copy-start | bytes 52
  2.6 1.0 %copy-start = (f32[1,128,1024]{2,1,0:T(8,128)S(1)}, f32[1,128,1024]{2,1,0:T(8,128)}, u32[]{:S(2)}) copy-start(f32[1,128,1024]{2,1,0:T(8,128)} %image_in.1) | copy-start | bytes 1572868
